TPU v7x, 32 devices: a whole 2x2x4 slice. The times are simulated.
32 devices in a mesh: grp: 2 (over x), ma: 16 (over z, y, core).
Axes of the slice: x: 2, y: 2, z: 4, core: 2. Of those that a mesh axis runs over, the one named last changes fastest.
Arguments:
- vis: float32 [16384, 2, 256], P(('grp', 'ma')), parts along dimension 0, may hold values from -6 to 6
- transfer: bfloat16 [32, 2, 256, 1024], P(('grp', 'ma')), parts along dimension 0, may hold values from -0.1875 to 0.1875
- band_start: int32 [2], P('grp'), parts along dimension 0, may hold values from 0 to 8176
- comp_index: int32 [2048], P(('grp', 'ma')), parts along dimension 0, may hold values from 0 to 16383
- comp_amp: int32 [2048, 2], P(('grp', 'ma')), parts along dimension 0, may hold values from -4096 to 4096
Outputs:
- residual_alm: float32 [32, 2, 1024], P(('grp', 'ma')), parts along dimension 0
There are 2 independent parts, one for each index of `grp`. A program takes and returns all parts, laid end to end along the dimension named above; each array names one. Nothing has to cross between parts.
All inputs are finite; a program needn't handle non-finite values.
Results may differ from a plain program's by a relative error of at most 0.003.
Values sent between devices are 32-bit elements; how exact they have to be, the bound alone decides.
No kernel may reach another device: no remote copies, remote signals or barrier semaphores. Data moves between devices by JAX's collectives and lax.ppermute only.
A program may use at most 64 MiB of HBM per device.

v0:
```python
import math
import jax
import jax.numpy as jnp
from jax import lax
from jax.sharding import PartitionSpec as P

SIDEREAL_TICKS = 8192


def trig_pair_lookup(azimuthal_orders, tick_moments):
    rotation_radians = azimuthal_orders[:, None] * tick_moments[None, :] % SIDEREAL_TICKS
    angle = rotation_radians.astype(jnp.float32) * (2.0 * math.pi / SIDEREAL_TICKS)
    return jnp.concatenate([jnp.cos(angle), jnp.sin(angle)], 0)


def combine_parts(product, row_count):
    product = product.reshape(2, row_count, 2, -1)
    scale = 1.0 / math.sqrt(SIDEREAL_TICKS)
    real_part = (product[0, :, 0] + product[1, :, 1]) * scale
    imag_part = (product[0, :, 1] - product[1, :, 0]) * scale
    return jnp.stack([real_part, imag_part], 1)


def body(vis, transfer, band_start, comp_index, comp_amp):
    ma_count = lax.axis_size("ma")
    device_rank = lax.axis_index("ma")
    m_local = transfer.shape[0]
    width = transfer.shape[3]
    modes = m_local * ma_count
    regrouped = lax.all_to_all(vis, "ma", split_axis=2, concat_axis=0, tiled=True)
    azimuthal_orders = band_start[0] + jnp.arange(modes, dtype=jnp.int32)
    trig_pair = trig_pair_lookup(azimuthal_orders, jnp.arange(SIDEREAL_TICKS, dtype=jnp.int32))
    flat_visibility = regrouped.reshape(SIDEREAL_TICKS, -1)
    product = jnp.dot(
        trig_pair,
        flat_visibility,
        precision=lax.Precision.HIGHEST,
        preferred_element_type=jnp.float32,
    )
    local_spectra = combine_parts(product, modes)
    spectra = lax.all_to_all(local_spectra, "ma", split_axis=0, concat_axis=2, tiled=True)
    index_all, amp_all = (
        lax.all_gather(comp_index, "ma", axis=0, tiled=True),
        lax.all_gather(comp_amp, "ma", axis=0, tiled=True),
    )
    slots = m_local * width
    offset = index_all - device_rank * slots
    inside = (offset >= 0) & (offset < slots)
    target = jnp.where(inside, offset, slots)
    summed = jax.ops.segment_sum(amp_all, target, num_segments=slots + 1)[:slots]
    model_alm = (
        (summed.astype(jnp.float32) * (1.0 / 1024.0))
        .astype(jnp.bfloat16)
        .reshape(m_local, width, 2)
    )
    predicted = jnp.einsum(
        "mcbl,mlk->mcbk", transfer, model_alm, preferred_element_type=jnp.float32
    )
    pred_real = predicted[:, 0, :, 0] - predicted[:, 1, :, 1]
    pred_imag = predicted[:, 0, :, 1] + predicted[:, 1, :, 0]
    resid_vis = (spectra - jnp.stack([pred_real, pred_imag], 1)).astype(jnp.bfloat16)
    projected = jnp.einsum(
        "mcbl,mkb->mkcl", transfer, resid_vis, preferred_element_type=jnp.float32
    )
    alm_real = projected[:, 0, 0] + projected[:, 1, 1]
    alm_imag = projected[:, 1, 0] - projected[:, 0, 1]
    return jnp.stack([alm_real, alm_imag], 1)


def solution(mesh):
    in_specs = (
        P(("grp", "ma"), None, None),
        P(("grp", "ma"), None, None, None),
        P("grp"),
        P(("grp", "ma")),
        P(("grp", "ma"), None),
    )
    out_specs = P(("grp", "ma"), None, None)
    return jax.shard_map(body, mesh=mesh, in_specs=in_specs, out_specs=out_specs, check_vma=False)
```

profile of v0, /device:TPU:0, one launch (start us, length us, event | category | flops | bytes accessed | tf_op | source)
XLA Modules:
  0.0 85.9 jit_solution(13697554280180083877)
XLA Ops:
  0.0 0.0 copy-start
  0.0 3.7 %copy.34 = f32[512,2,256]{0,1,2:T(2,128)} copy(f32[512,2,256]{2,1,0:T(2,128)} %param.5) | data formatting | bytes 2097152 | tf_op args[0]
  3.7 7.4 %all-to-all-start = ((f32[512,2,256]{0,1,2:T(2,128)}), f32[512,2,256]{0,1,2:T(2,128)S(1)}, u32[]{:S(2)}, u32[]{:S(2)}) async-start(f32[512,2,256]{0,1,2:T(2,128)} %copy.34), calls=%async_computation | async-start | bytes 2097152 | tf_op jit(solution)/shard_map/all_to_all | solution.py:30
  11.8 0.0 copy-start.3
  11.8 0.6 copy-done.3
  12.5 0.6 dynamic-slice
  13.7 0.0 copy-start.2
  13.7 0.6 copy-done.2
  14.4 0.2 dynamic-update-slice
  14.5 23.3 %all-reduce = s32[1024]{0:T(1024)S(1)} all-reduce(s32[1024]{0:T(1024)S(1)} %dynamic-update-slice), channel_id=1, replica_groups=mesh['grp'=2,'ma'=16] {'ma'}, use_global_device_ids=true, to_apply=%add | all-reduce | flops 1024 | bytes 8192
  37.8 0.0 copy-start.1
  37.8 0.7 copy-done.1
  38.5 19.5 %all-gather = s32[16,64,2]{1,2,0:T(2,128)S(1)} all-gather(s32[1,64,2]{1,2,0:T(2,128)S(1)} %bitcast.60), channel_id=1, replica_groups=mesh['grp'=2,'ma'=16] {'ma'}, dimensions={0}, use_global_device_ids=true | all-gather | bytes 8704 | tf_op jit(solution)/shard_map/all_gather | solution.py:44
  58.0 0.2 copy.43
  58.2 7.4 %scatter_custom_fusion = s32[1025,2]{1,0:T(8,128)S(1)} fusion(s32[1024]{0:T(1024)S(1)} %and_select_fusion, s32[1024,2]{1,0:T(8,128)S(1)} %bitcast.59, s32[]{:T(128)} %constant.9.clone.1), kind=kCustom, calls=%fused_computation.16 | custom fusion | flops 2048 | bytes 8204 | tf_op jit(solution)/shard_map/scatter-add | solution.py:50
  65.7 0.1 multiply_convert_fusion
  65.7 0.1 copy.47
  65.9 0.0 copy-done
  65.9 0.4 convolution_bitcast_fusion.1
  66.2 2.1 %fusion.11 = (f32[16,8192]{1,0:T(8,128)S(1)}, f32[16,8192]{1,0:T(8,128)S(1)}) fusion(s32[16]{0:T(128)S(1)} %iota_add_fusion), kind=kLoop, calls=%fused_computation.19 | loop fusion | flops 1835008 | bytes 1048640 | tf_op jit(solution)/shard_map/cos | solution.py:13
  68.4 0.1 pad_maximum_fusion
  68.5 0.0 all-to-all-done
  68.5 0.2 copy.35
  68.7 0.6 copy.36
  69.3 0.6 copy.46
  69.9 4.4 %fusion.22 = f32[2,16,2,16]{3,1,2,0:T(8,128)S(1)} fusion(f32[2,16,8192,1]{2,1,3,0:T(8,128)S(1)} %bitcast.55, f32[2,16,8192,1]{2,1,0,3:T(8,128)S(1)} %bitcast.56), kind=kOutput, calls=%fused_computation.41 | convolution fusion | flops 100663296 | bytes 2101248 | tf_op jit(solution)/shard_map/dot_general | solution.py:34
  74.4 0.6 copy.37
  75.0 3.5 %all-to-all-start.1 = ((f32[16,2,16]{2,1,0:T(2,128)}), f32[16,2,16]{2,1,0:T(2,128)S(1)}, u32[]{:S(2)}, u32[]{:S(2)}) async-start(f32[16,2,16]{2,1,0:T(2,128)} %copy.37), calls=%async_computation.1 | async-start | bytes 32768 | tf_op jit(solution)/shard_map/all_to_all | solution.py:41
  78.5 0.1 add.66
  78.6 0.1 sub.60
  78.6 6.3 %all-to-all-done.1 = f32[16,2,16]{2,1,0:T(2,128)S(1)} async-done(((f32[16,2,16]{2,1,0:T(2,128)}), f32[16,2,16]{2,1,0:T(2,128)S(1)}, u32[]{:S(2)}, u32[]{:S(2)}) %all-to-all-start.1) | async-done | bytes 2080 | tf_op jit(solution)/shard_map/all_to_all | solution.py:41
  84.9 0.1 reshape.206
  85.0 0.2 convolution_bitcast_fusion
  85.3 0.6 pad_maximum_fusion.2
  (8 shorter events, 0.1 us)
Async XLA Ops:
  0.0 65.9 %copy-start = (bf16[1,2,256,1024]{3,2,1,0:T(8,128)(2,1)S(1)}, bf16[1,2,256,1024]{3,2,1,0:T(8,128)(2,1)}, u32[]{:S(2)}) copy-start(bf16[1,2,256,1024]{3,2,1,0:T(8,128)(2,1)} %param.6) | copy-start | bytes 3145732
  3.7 64.7 %all-to-all-start = ((f32[512,2,256]{0,1,2:T(2,128)}), f32[512,2,256]{0,1,2:T(2,128)S(1)}, u32[]{:S(2)}, u32[]{:S(2)}) async-start(f32[512,2,256]{0,1,2:T(2,128)} %copy.34), calls=%async_computation | async-start | bytes 2097152 | tf_op jit(solution)/shard_map/all_to_all | solution.py:30
  11.8 0.7 copy-start.3
  13.7 0.7 copy-start.2
  37.8 0.7 copy-start.1
  75.0 9.9 %all-to-all-start.1 = ((f32[16,2,16]{2,1,0:T(2,128)}), f32[16,2,16]{2,1,0:T(2,128)S(1)}, u32[]{:S(2)}, u32[]{:S(2)}) async-start(f32[16,2,16]{2,1,0:T(2,128)} %copy.37), calls=%async_computation.1 | async-start | bytes 32768 | tf_op jit(solution)/shard_map/all_to_all | solution.py:41
where the time goes:
time: 86.3 us; the launch traced here: 85.9 us
  blocking collectives  42.8 us (50%)
  starting transfers between devices  10.9 us (13%)
  other arithmetic  10.3 us (12%)
  local copies, waits for them, and re-layouts  9.1 us (11%)
  waiting for transfers between devices  6.29 us (7%)
  matrix products  5.05 us (6%)
  between operations  1.48 us (2%)
    unnamed x1, blocking collectives  23.3 us
    all_gather x1, blocking collectives, body(): lax.all_gather(comp_amp, 'ma', axis=0, tiled=True)  19.5 us
    unnamed x15, local copies, waits for them, and re-layouts  7.42 us
    all_to_all x1, starting transfers between devices, body(): lax.all_to_all(vis, 'ma', split_axis=2, concat_axis=0, tiled=True)  7.41 us
    scatter-add x1, other arithmetic, body(): jax.ops.segment_sum(amp_all, target, num_segments=slots + 1)[:slots]  7.41 us
    all_to_all x1, waiting for transfers between devices, body(): lax.all_to_all(local_spectra, 'ma', split_axis=0, concat_axis=2, tiled=True)  6.28 us
    dot_general x1, matrix products, body(): jnp.dot(trig_pair, flat_visibility, precision=lax.Precision.HIGHEST, pref...  4.42 us
    all_to_all x1, starting transfers between devices, body(): lax.all_to_all(local_spectra, 'ma', split_axis=0, concat_axis=2, tiled=True)  3.47 us
  transfers between devices with their start and end apart: 2, of which 1 were waited for; matrix products, arithmetic and copies ran while one was open for 13% of the time, Pallas kernels for 0%

commit v1 on v0

--- a/solution.py
+++ b/solution.py
@@ -1,3 +1,4 @@
+import functools
 import math
 import jax
 import jax.numpy as jnp
@@ -5,6 +6,17 @@
 from jax.sharding import PartitionSpec as P
 
 SIDEREAL_TICKS = 8192
+
+
+def pass_the_plate(point, across):
+    d_next = tuple((point for _ in range(jax.lax.axis_size(across))))
+    before = jnp.stack(d_next, 0)
+    z_new = jax.lax.all_to_all(before, axis_name=across, split_axis=0, concat_axis=0)
+    prior = jnp.concatenate(z_new, 0)
+    return prior
+
+
+skins_enter = functools.partial(pass_the_plate, across="ma")
 
 
 def trig_pair_lookup(azimuthal_orders, tick_moments):
@@ -41,7 +53,7 @@
     spectra = lax.all_to_all(local_spectra, "ma", split_axis=0, concat_axis=2, tiled=True)
     index_all, amp_all = (
         lax.all_gather(comp_index, "ma", axis=0, tiled=True),
-        lax.all_gather(comp_amp, "ma", axis=0, tiled=True),
+        skins_enter(comp_amp),
     )
     slots = m_local * width
     offset = index_all - device_rank * slots

time: 86.3 us -> 77.7 us (0.900)
  blocking collectives: 42.8 us -> 20.7 us
  other arithmetic: 10.3 us -> 15.5 us
  starting transfers between devices: 10.9 us -> 14.9 us
  waiting for transfers between devices: 6.29 us -> 8.41 us
  local copies, waits for them, and re-layouts: 9.1 us -> 11.2 us
    all_gather x1 -> x0, blocking collectives: 19.5 us -> none  [body(): lax.all_gather(comp_amp, 'ma', axis=0, tiled=True)]
    all_to_all x0 -> x1, starting transfers between devices: none -> 7.41 us  [pass_the_plate(): jax.lax.all_to_all(before, axis_name=across, split_axis=0, concat_axis=0)]
    all_to_all x1, starting transfers between devices: 7.41 us -> 3.94 us  [body(): lax.all_to_all(vis, 'ma', split_axis=2, concat_axis=0, tiled=True)]
    unnamed x1, blocking collectives: 23.3 us -> 20.7 us
    all_to_all x0 -> x1, waiting for transfers between devices: none -> 2.08 us  [pass_the_plate(): jax.lax.all_to_all(before, axis_name=across, split_axis=0, concat_axis=0)]
    concatenate x1, other arithmetic: 0.07 us -> 1.27 us  [trig_pair_lookup(): return jnp.concatenate([jnp.cos(angle), jnp.sin(angle)], 0)]
    cos x1, other arithmetic: 2.13 us -> 3.26 us  [trig_pair_lookup(): return jnp.concatenate([jnp.cos(angle), jnp.sin(angle)], 0)]
    scatter-add x1, other arithmetic: 7.41 us -> 8.52 us  [body(): jax.ops.segment_sum(amp_all, target, num_segments=slots + 1)[:slots]]
  transfers between devices with their start and end apart: 2 -> 3, of which waited for: 1 -> 2; matrix products, arithmetic and copies ran while one was open for 13% -> 28% of each run, Pallas kernels for 0% -> 0%
where the time goes in v1:
time: 77.7 us; the launch traced here: 77.2 us
  blocking collectives  20.7 us (27%)
  other arithmetic  15.5 us (20%)
  starting transfers between devices  14.9 us (19%)
  local copies, waits for them, and re-layouts  11.2 us (14%)
  waiting for transfers between devices  8.41 us (11%)
  matrix products  5.05 us (6%)
  between operations  1.43 us (2%)
    unnamed x1, blocking collectives  20.7 us
    scatter-add x1, other arithmetic, body(): jax.ops.segment_sum(amp_all, target, num_segments=slots + 1)[:slots]  8.52 us
    unnamed x15, local copies, waits for them, and re-layouts  7.96 us
    all_to_all x1, starting transfers between devices, pass_the_plate(): jax.lax.all_to_all(before, axis_name=across, split_axis=0, concat_axis=0)  7.41 us
    all_to_all x1, waiting for transfers between devices, body(): lax.all_to_all(local_spectra, 'ma', split_axis=0, concat_axis=2, tiled=True)  6.32 us
    dot_general x1, matrix products, body(): jnp.dot(trig_pair, flat_visibility, precision=lax.Precision.HIGHEST, pref...  4.42 us
    all_to_all x1, starting transfers between devices, body(): lax.all_to_all(vis, 'ma', split_axis=2, concat_axis=0, tiled=True)  3.94 us
    all_to_all x1, starting transfers between devices, body(): lax.all_to_all(local_spectra, 'ma', split_axis=0, concat_axis=2, tiled=True)  3.58 us
  transfers between devices with their start and end apart: 3, of which 2 were waited for; matrix products, arithmetic and copies ran while one was open for 28% of the time, Pallas kernels for 0%

profile of v1, /device:TPU:0, one launch (start us, length us, event | category | flops | bytes accessed | tf_op | source)
XLA Modules:
  0.0 77.2 jit_solution(13121800190383370915)
XLA Ops:
  0.0 0.0 copy-start
  0.0 0.8 broadcast_bitcast_fusion
  0.8 0.7 reshape.226
  1.5 7.4 %all-to-all-start.2 = ((s32[16,1,128]{2,1,0:T(1,128)}), s32[16,1,128]{2,1,0:T(1,128)S(1)}, u32[]{:S(2)}, u32[]{:S(2)}) async-start(s32[16,1,128]{2,1,0:T(1,128)} %reshape.226), calls=%async_computation.2 | async-start | bytes 16384 | tf_op jit(solution)/shard_map/all_to_all | solution.py:14
  9.5 3.6 %copy.31 = f32[512,2,256]{0,1,2:T(2,128)} copy(f32[512,2,256]{2,1,0:T(2,128)} %param.5) | data formatting | bytes 2097152 | tf_op args[0]
  13.2 2.1 %all-to-all-done.2 = s32[16,1,128]{2,1,0:T(1,128)S(1)} async-done(((s32[16,1,128]{2,1,0:T(1,128)}), s32[16,1,128]{2,1,0:T(1,128)S(1)}, u32[]{:S(2)}, u32[]{:S(2)}) %all-to-all-start.2) | async-done | bytes 8224 | tf_op jit(solution)/shard_map/all_to_all | solution.py:14
  15.2 3.9 %all-to-all-start = ((f32[512,2,256]{0,1,2:T(2,128)}), f32[512,2,256]{0,1,2:T(2,128)S(1)}, u32[]{:S(2)}, u32[]{:S(2)}) async-start(f32[512,2,256]{0,1,2:T(2,128)} %copy.31), calls=%async_computation | async-start | bytes 2097152 | tf_op jit(solution)/shard_map/all_to_all | solution.py:42
  19.2 3.3 %fusion.11 = (f32[16,8192]{1,0:T(8,128)}, f32[16,8192]{1,0:T(8,128)}) fusion(s32[16]{0:T(128)S(1)} %iota_add_fusion), kind=kLoop, calls=%fused_computation.19 | loop fusion | flops 1835008 | bytes 1048640 | tf_op jit(solution)/shard_map/cos | solution.py:25
  22.5 0.0 copy-start.2
  22.5 0.7 copy-done.2
  23.1 0.6 dynamic-slice
  24.3 0.0 copy-start.1
  24.4 0.6 copy-done.1
  25.0 0.2 dynamic-update-slice
  25.2 20.7 %all-reduce = s32[1024]{0:T(1024)S(1)} all-reduce(s32[1024]{0:T(1024)S(1)} %dynamic-update-slice), channel_id=1, replica_groups=mesh['grp'=2,'ma'=16] {'ma'}, use_global_device_ids=true, to_apply=%add | all-reduce | flops 1024 | bytes 8192
  45.9 1.3 %pad_maximum_fusion = f32[32,8192]{1,0:T(8,128)S(1)} fusion(f32[16,8192]{1,0:T(8,128)} %get-tuple-element.12, f32[16,8192]{1,0:T(8,128)} %get-tuple-element.11), kind=kLoop, calls=%fused_computation.3 | loop fusion | flops 262144 | bytes 2097152 | tf_op jit(solution)/shard_map/concatenate | solution.py:25
  47.2 0.5 broadcast.51
  47.7 0.7 reduce.8
  48.4 0.1 reshape.227
  48.4 1.1 %copy.40 = s32[16,64,2]{2,1,0:T(8,128)} copy(s32[16,64,2]{1,2,0:T(2,128)S(1)} %bitcast.62) | data formatting | bytes 16384 | tf_op jit(solution)/shard_map/reshape | solution.py:15
  49.5 8.5 %scatter_custom_fusion = s32[1025,2]{1,0:T(8,128)} fusion(s32[1024]{0:T(1024)S(1)} %and_select_fusion, s32[1024,2]{1,0:T(8,128)} %bitcast.61, s32[]{:T(128)} %constant.9.clone.1), kind=kCustom, calls=%fused_computation.16 | custom fusion | flops 2048 | bytes 8712 | tf_op jit(solution)/shard_map/scatter-add | solution.py:62
  58.0 1.1 %multiply_convert_fusion = bf16[1024,2]{1,0:T(8,128)(2,1)S(1)} fusion(s32[1025,2]{1,0:T(8,128)} %scatter_custom_fusion), kind=kLoop, calls=%fused_computation.12 | loop fusion | flops 6144 | bytes 12288 | tf_op jit(solution)/shard_map/convert_element_type | solution.py:65
  59.1 0.1 copy.44
  59.2 0.0 copy-done
  59.3 0.4 convolution_bitcast_fusion.1
  59.6 0.0 all-to-all-done
  59.6 0.2 copy.32
  59.9 0.6 copy.33
  60.5 0.6 copy.43
  61.1 4.4 %fusion.22 = f32[2,16,2,16]{3,1,2,0:T(8,128)S(1)} fusion(f32[2,16,8192,1]{2,1,3,0:T(8,128)S(1)} %bitcast.57, f32[2,16,8192,1]{2,1,0,3:T(8,128)S(1)} %bitcast.58), kind=kOutput, calls=%fused_computation.42 | convolution fusion | flops 100663296 | bytes 2101248 | tf_op jit(solution)/shard_map/dot_general | solution.py:46
  65.6 0.6 copy.34
  66.2 3.6 %all-to-all-start.1 = ((f32[16,2,16]{2,1,0:T(2,128)}), f32[16,2,16]{2,1,0:T(2,128)S(1)}, u32[]{:S(2)}, u32[]{:S(2)}) async-start(f32[16,2,16]{2,1,0:T(2,128)} %copy.34), calls=%async_computation.1 | async-start | bytes 32768 | tf_op jit(solution)/shard_map/all_to_all | solution.py:53
  69.8 0.1 add.66
  69.9 0.1 sub.60
  69.9 6.3 %all-to-all-done.1 = f32[16,2,16]{2,1,0:T(2,128)S(1)} async-done(((f32[16,2,16]{2,1,0:T(2,128)}), f32[16,2,16]{2,1,0:T(2,128)S(1)}, u32[]{:S(2)}, u32[]{:S(2)}) %all-to-all-start.1) | async-done | bytes 2080 | tf_op jit(solution)/shard_map/all_to_all | solution.py:53
  76.3 0.1 reshape.210
  76.4 0.2 convolution_bitcast_fusion
  76.6 0.6 pad_maximum_fusion.2
  (8 shorter events, 0.1 us)
Async XLA Ops:
  0.0 59.3 %copy-start = (bf16[1,2,256,1024]{3,2,1,0:T(8,128)(2,1)S(1)}, bf16[1,2,256,1024]{3,2,1,0:T(8,128)(2,1)}, u32[]{:S(2)}) copy-start(bf16[1,2,256,1024]{3,2,1,0:T(8,128)(2,1)} %param.6) | copy-start | bytes 3145732
  1.5 13.8 %all-to-all-start.2 = ((s32[16,1,128]{2,1,0:T(1,128)}), s32[16,1,128]{2,1,0:T(1,128)S(1)}, u32[]{:S(2)}, u32[]{:S(2)}) async-start(s32[16,1,128]{2,1,0:T(1,128)} %reshape.226), calls=%async_computation.2 | async-start | bytes 16384 | tf_op jit(solution)/shard_map/all_to_all | solution.py:14
  15.2 44.4 %all-to-all-start = ((f32[512,2,256]{0,1,2:T(2,128)}), f32[512,2,256]{0,1,2:T(2,128)S(1)}, u32[]{:S(2)}, u32[]{:S(2)}) async-start(f32[512,2,256]{0,1,2:T(2,128)} %copy.31), calls=%async_computation | async-start | bytes 2097152 | tf_op jit(solution)/shard_map/all_to_all | solution.py:42
  22.5 0.7 copy-start.2
  24.3 0.7 copy-start.1
  66.2 10.1 %all-to-all-start.1 = ((f32[16,2,16]{2,1,0:T(2,128)}), f32[16,2,16]{2,1,0:T(2,128)S(1)}, u32[]{:S(2)}, u32[]{:S(2)}) async-start(f32[16,2,16]{2,1,0:T(2,128)} %copy.34), calls=%async_computation.1 | async-start | bytes 32768 | tf_op jit(solution)/shard_map/all_to_all | solution.py:53
